TPU v7x, 512 devices: a whole 4x8x8 slice. The times are simulated.
512 devices in a mesh: vox: 32 (over z_lo, y), opt: 16 (over z_hi, x, core).
Axes of the slice: x: 4, y: 8, z: 8 (z_hi: 2, z_lo: 4; z = z_hi * 4 + z_lo), core: 2. Of those that a mesh axis runs over, the one named last changes fastest.
Arguments:
- source_fields: bfloat16 [1024, 24576], P('opt', 'vox'), may hold values from -6 to 6
- detector_fields: bfloat16 [4096, 24576], P('opt', 'vox'), may hold values from -6 to 6
- measured: float32 [1024, 4096], P('vox', 'opt'), may hold values from -6 to 6
- valid_pair: int32 [1024, 4096], P('vox', 'opt'), may hold values 0 or 1
- weight_class: int32 [1024, 4096], P('vox', 'opt'), may hold values from 0 to 3
- absorption: float32 [24576], P('vox'), may hold values from 0 to 1
Outputs:
- absorption_out: float32 [24576], P('vox')
- residual_out: float32 [1024, 4096], P('vox', 'opt')
All inputs are finite; a program needn't handle non-finite values. No bound on the sum of `valid_pair` on one device may be relied on, other than what follows from the above.
Results may differ from a plain program's by a relative error of at most 0.0026.
Values may be sent and summed in bfloat16 or wider, within the bound.
No kernel may reach another device: no remote copies, remote signals or barrier semaphores. Data moves between devices by JAX's collectives and lax.ppermute only.
A program may use at most 64 MiB of HBM per device.

v0:
```python
import jax
import jax.numpy as jnp
from jax import lax
from jax.sharding import PartitionSpec as P

NS = 1024
ND = 4096
ITERS = 2


def local(source_fields, detector_fields, measured, valid_pair, weight_class, absorption):
    vox_count = lax.axis_size("vox")
    voxels = absorption.shape[0] * vox_count
    pred_scale = 1.0 / jnp.sqrt(jnp.float32(voxels))
    grad_scale = jnp.sqrt(jnp.float32(voxels)) / (jnp.float32(NS) * jnp.float32(ND))
    own_rows = measured.shape[0]
    maskf = valid_pair.astype(jnp.float32) / (1.0 + weight_class.astype(jnp.float32))
    mu_now = absorption
    weighted = jnp.zeros(measured.shape, jnp.float32)
    for step in range(ITERS):
        scaled = (detector_fields * mu_now[None, :]).astype(jnp.bfloat16)
        partial_pred = lax.dot_general(
            lax.all_gather(source_fields, "opt", axis=0, tiled=True),
            scaled,
            (((1,), (1,)), ((), ())),
            preferred_element_type=jnp.float32,
        )
        summed = lax.psum(partial_pred, "vox")
        predicted = lax.dynamic_slice_in_dim(summed, lax.axis_index("vox") * own_rows, own_rows, 0)
        weighted = maskf * (predicted * pred_scale - measured)
        weighted_b = weighted.astype(jnp.bfloat16)
        inner = jnp.dot(
            lax.all_gather(weighted_b, "vox", axis=0, tiled=True),
            detector_fields,
            preferred_element_type=jnp.float32,
        )
        local_grad = jnp.sum(
            inner * lax.all_gather(source_fields, "opt", axis=0, tiled=True), axis=0
        )
        gradient = lax.psum(local_grad, "opt") * grad_scale
        mu_now = jnp.maximum(mu_now - 2.0 * gradient, 0.0)
    return (mu_now, weighted)


def solution(mesh):
    placed = (
        P("opt", "vox"),
        P("opt", "vox"),
        P("vox", "opt"),
        P("vox", "opt"),
        P("vox", "opt"),
        P("vox"),
    )
    return jax.shard_map(
        local, mesh=mesh, in_specs=placed, out_specs=(P("vox"), P("vox", "opt")), check_vma=False
    )
```

profile of v0, /device:TPU:1, one launch (start us, length us, event | category | flops | bytes accessed | tf_op | source)
XLA Modules:
  0.0 953.0 jit_solution(11896403717239012675)
XLA Ops:
  7.2 0.0 all-gather.2.cloned.1.call-start
  7.2 0.7 all-gather.2.cloned.1.call-update
  7.9 0.0 all-reduce.3.cloned.1.call-start
  8.0 74.2 %all-gather.2.cloned.1.call-done = bf16[1024,768]{1,0:T(8,128)(2,1)} async-done(((bf16[64,768]{1,0:T(8,128)(2,1)}), bf16[1024,768]{1,0:T(8,128)(2,1)}) %all-gather.2.cloned.1.call-update) | async-done | bytes 1572880 | tf_op jit(solution)/shard_map/all_gather | solution.py:23
  82.2 3.2 convolution_bitcast_fusion.1
  85.4 0.0 all-reduce.3.cloned.1.call-update
  85.4 0.0 all-reduce.5.cloned.1.call-start
  85.5 284.5 %all-reduce.3.cloned.1.call-done = f32[1024,256]{1,0:T(8,128)} async-done(((f32[1024,256]{1,0:T(8,128)}), f32[1024,256]{1,0:T(8,128)}) %all-reduce.3.cloned.1.call-update) | async-done | bytes 1048592 | tf_op jit(solution)/shard_map/psum | solution.py:28
  370.0 0.0 copy-done.2
  370.0 0.0 copy-done.4
  370.0 0.8 multiply_convert_fusion
  370.8 66.8 %all_gather.13 = bf16[1024,256]{1,0:T(8,128)(2,1)S(1)} all-gather(bf16[32,256]{1,0:T(8,128)(2,1)S(1)} %multiply_convert_fusion), channel_id=1, replica_groups=mesh['vox'=32,'opt'=16] {'vox'}, dimensions={0}, use_global_device_ids=true | all-gather | bytes 540672 | tf_op jit(solution)/shard_map/all_gather | solution.py:33
  437.6 0.0 copy-done
  437.6 0.6 fusion
  438.2 78.6 %psum.29 = f32[768]{0:T(1024)S(1)} all-reduce(f32[768]{0:T(1024)S(1)} %fusion), channel_id=1, replica_groups=mesh['vox'=32,'opt'=16] {'opt'}, use_global_device_ids=true, to_apply=%region_2.0 | all-reduce | flops 768 | bytes 6144 | tf_op jit(solution)/shard_map/psum | solution.py:40
  516.8 0.0 copy-done.5
  516.8 1.6 convolution_bitcast_fusion
  518.5 0.0 all-reduce.5.cloned.1.call-update
  518.5 280.0 %all-reduce.5.cloned.1.call-done = f32[1024,256]{1,0:T(8,128)} async-done(((f32[1024,256]{1,0:T(8,128)}), f32[1024,256]{1,0:T(8,128)}) %all-reduce.5.cloned.1.call-update) | async-done | bytes 1048592 | tf_op jit(solution)/shard_map/psum | solution.py:28
  798.5 1.4 fusion.8
  799.9 65.8 %all_gather.14 = bf16[1024,256]{1,0:T(8,128)(2,1)S(1)} all-gather(bf16[32,256]{1,0:T(8,128)(2,1)S(1)} %get-tuple-element.6), channel_id=1, replica_groups=mesh['vox'=32,'opt'=16] {'vox'}, dimensions={0}, use_global_device_ids=true | all-gather | bytes 540672 | tf_op jit(solution)/shard_map/all_gather | solution.py:33
  865.7 0.6 fusion.1
  866.4 79.5 %psum.31 = f32[768]{0:T(1024)S(1)} all-reduce(f32[768]{0:T(1024)S(1)} %fusion.1), channel_id=1, replica_groups=mesh['vox'=32,'opt'=16] {'opt'}, use_global_device_ids=true, to_apply=%region_5.0 | all-reduce | flops 768 | bytes 6144 | tf_op jit(solution)/shard_map/psum | solution.py:40
  945.8 0.6 subtract_maximum_fusion
  (9 shorter events, 0.0 us)
Async XLA Ops:
  7.2 75.0 %all-gather.2.cloned.1.call-start = ((), (), s32[]{:S(2)}) async-start(), calls=%async_computation | async-start | bytes 1671168 | tf_op jit(solution)/shard_map/all_gather | solution.py:23
  7.9 362.1 %copy-start.2 = (f32[32,256]{1,0:T(8,128)S(1)}, f32[32,256]{1,0:T(8,128)}, u32[]{:S(2)}) copy-start(f32[32,256]{1,0:T(8,128)} %param.8) | copy-start | bytes 98308
  7.9 362.1 %copy-start.3 = (s32[32,256]{1,0:T(8,128)S(1)}, s32[32,256]{1,0:T(8,128)}, u32[]{:S(2)}) copy-start(s32[32,256]{1,0:T(8,128)} %param.10) | copy-start | bytes 98308
  7.9 362.1 %copy-start.4 = (s32[32,256]{1,0:T(8,128)S(1)}, s32[32,256]{1,0:T(8,128)}, u32[]{:S(2)}) copy-start(s32[32,256]{1,0:T(8,128)} %param.9) | copy-start | bytes 98308
  7.9 362.1 %all-reduce.3.cloned.1.call-start = ((), (), s32[]{:S(2)}) async-start(), calls=%async_computation.1 | async-start | bytes 2097152 | tf_op jit(solution)/shard_map/psum | solution.py:28
  82.2 355.4 %copy-start.1 = (bf16[256,768]{1,0:T(8,128)(2,1)S(1)}, bf16[256,768]{1,0:T(8,128)(2,1)}, u32[]{:S(2)}) copy-start(bf16[256,768]{1,0:T(8,128)(2,1)} %param.7) | copy-start | bytes 1179652
  85.4 352.2 %copy-start = (bf16[1024,768]{1,0:T(8,128)(2,1)S(1)}, bf16[1024,768]{1,0:T(8,128)(2,1)}, u32[]{:S(2)}) copy-start(bf16[1024,768]{1,0:T(8,128)(2,1)} %all-gather.2.cloned.1.call-done) | copy-start | bytes 4718596
  85.4 713.1 %all-reduce.5.cloned.1.call-start = ((), (), s32[]{:S(2)}) async-start(), calls=%async_computation.2 | async-start | bytes 2097152 | tf_op jit(solution)/shard_map/psum | solution.py:28
  437.6 79.2 %copy-start.5 = (f32[768]{0:T(1024)S(1)}, f32[768]{0:T(1024)}, u32[]{:S(2)}) copy-start(f32[768]{0:T(1024)} %param.11) | copy-start | bytes 9220
Sparse Core Ops, SparseCore 0:
  11.3 70.8 all-gather.1
  85.5 284.4 all-reduce.2
  518.6 279.8 all-reduce.4
where the time goes:
time: 953 us
  waiting for transfers between devices  639 us (67%)
  blocking collectives  291 us (31%)
  between operations  13.8 us (1%)
    psum x2, waiting for transfers between devices, local(): summed = lax.psum(partial_pred, 'vox')  565 us
    psum x2, blocking collectives, local(): gradient = lax.psum(local_grad, 'opt') * grad_scale  158 us
    all_gather x2, blocking collectives, local(): lax.all_gather(weighted_b, 'vox', axis=0, tiled=True)  133 us
    all_gather x1, waiting for transfers between devices, local(): lax.all_gather(source_fields, 'opt', axis=0, tiled=True)  74.2 us
  transfers between devices with their start and end apart: 3, of which 3 were waited for; matrix products, arithmetic and copies ran while one was open for 0% of the time, Pallas kernels for 0%

commit v1 on v0

--- a/solution.py
+++ b/solution.py
@@ -20,7 +20,10 @@
     for step in range(ITERS):
         scaled = (detector_fields * mu_now[None, :]).astype(jnp.bfloat16)
         partial_pred = lax.dot_general(
-            lax.all_gather(source_fields, "opt", axis=0, tiled=True),
+            jnp.concatenate(
+                lax.all_to_all(jnp.stack([source_fields] * lax.axis_size("opt")), "opt", 0, 0),
+                axis=0,
+            ),
             scaled,
             (((1,), (1,)), ((), ())),
             preferred_element_type=jnp.float32,

time: 953 us -> 940 us (0.986)
  waiting for transfers between devices: 639 us -> 583 us
  blocking collectives: 291 us -> 330 us
    all_gather x1, waiting for transfers between devices: 74.2 us -> 0.01 us  [local(): lax.all_gather(source_fields, 'opt', axis=0, tiled=True)]
    all_to_all x0 -> x1, blocking collectives: none -> 39.3 us  [local(): lax.all_to_all(jnp.stack([source_fields] * lax.axis_size('opt')), 'opt',...]
    psum x2, waiting for transfers between devices: 565 us -> 583 us  [local(): summed = lax.psum(partial_pred, 'vox')]
  transfers between devices with their start and end apart: 3 -> 3, of which waited for: 3 -> 2; matrix products, arithmetic and copies ran while one was open for 0% -> 0% of each run, Pallas kernels for 0% -> 0%
where the time goes in v1:
time: 940 us
  waiting for transfers between devices  583 us (62%)
  blocking collectives  330 us (35%)
  between operations  15.6 us (2%)
    psum x2, waiting for transfers between devices, local(): summed = lax.psum(partial_pred, 'vox')  583 us
    psum x2, blocking collectives, local(): gradient = lax.psum(local_grad, 'opt') * grad_scale  158 us
    all_gather x2, blocking collectives, local(): lax.all_gather(weighted_b, 'vox', axis=0, tiled=True)  133 us
    all_to_all x1, blocking collectives, local(): lax.all_to_all(jnp.stack([source_fields] * lax.axis_size('opt')), 'opt',...  39.3 us
  transfers between devices with their start and end apart: 3, of which 2 were waited for; matrix products, arithmetic and copies ran while one was open for 0% of the time, Pallas kernels for 0%

profile of v1, /device:TPU:1, one launch (start us, length us, event | category | flops | bytes accessed | tf_op | source)
XLA Modules:
  0.0 939.9 jit_solution(10117470338385089969)
XLA Ops:
  8.0 0.0 all-reduce.3.cloned.1.call-start
  8.0 1.0 stack.2
  9.1 0.0 copy-start
  9.1 0.0 copy-start.4
  9.1 39.3 %all_to_all.6 = bf16[16,64,768]{2,1,0:T(8,128)(2,1)S(1)} all-to-all(bf16[16,64,768]{2,1,0:T(8,128)(2,1)S(1)} %stack.2), channel_id=1, replica_groups=mesh['vox'=32,'opt'=16] {'opt'}, dimensions={0} | all-to-all | bytes 3145728 | tf_op jit(solution)/shard_map/all_to_all | solution.py:24
  48.4 0.0 copy-start.3
  48.4 1.6 convolution_bitcast_fusion.1
  50.0 0.0 all-reduce.3.cloned.1.call-update
  50.0 0.0 all-gather.2.cloned.1.call-start
  50.1 0.5 all-gather.2.cloned.1.call-update
  50.6 0.0 all-reduce.5.cloned.1.call-start
  50.7 302.6 %all-reduce.3.cloned.1.call-done = f32[1024,256]{1,0:T(8,128)} async-done(((f32[1024,256]{1,0:T(8,128)}), f32[1024,256]{1,0:T(8,128)}) %all-reduce.3.cloned.1.call-update) | async-done | bytes 1048592 | tf_op jit(solution)/shard_map/psum | solution.py:31
  353.3 0.8 multiply_convert_fusion
  354.1 66.8 %all_gather.10 = bf16[1024,256]{1,0:T(8,128)(2,1)S(1)} all-gather(bf16[32,256]{1,0:T(8,128)(2,1)S(1)} %multiply_convert_fusion), channel_id=1, replica_groups=mesh['vox'=32,'opt'=16] {'vox'}, dimensions={0}, use_global_device_ids=true | all-gather | bytes 540672 | tf_op jit(solution)/shard_map/all_gather | solution.py:36
  420.8 2.0 fusion
  422.9 78.6 %psum.29 = f32[768]{0:T(1024)S(1)} all-reduce(f32[768]{0:T(1024)S(1)} %fusion), channel_id=1, replica_groups=mesh['vox'=32,'opt'=16] {'opt'}, use_global_device_ids=true, to_apply=%region_2.0 | all-reduce | flops 768 | bytes 6144 | tf_op jit(solution)/shard_map/psum | solution.py:43
  501.5 1.6 convolution_bitcast_fusion
  503.1 0.0 all-reduce.5.cloned.1.call-update
  503.1 280.0 %all-reduce.5.cloned.1.call-done = f32[1024,256]{1,0:T(8,128)} async-done(((f32[1024,256]{1,0:T(8,128)}), f32[1024,256]{1,0:T(8,128)}) %all-reduce.5.cloned.1.call-update) | async-done | bytes 1048592 | tf_op jit(solution)/shard_map/psum | solution.py:31
  783.2 1.4 fusion.8
  784.5 65.8 %all_gather.12 = bf16[1024,256]{1,0:T(8,128)(2,1)S(1)} all-gather(bf16[32,256]{1,0:T(8,128)(2,1)S(1)} %get-tuple-element.6), channel_id=1, replica_groups=mesh['vox'=32,'opt'=16] {'vox'}, dimensions={0}, use_global_device_ids=true | all-gather | bytes 540672 | tf_op jit(solution)/shard_map/all_gather | solution.py:36
  850.4 2.0 fusion.1
  852.4 79.5 %psum.31 = f32[768]{0:T(1024)S(1)} all-reduce(f32[768]{0:T(1024)S(1)} %fusion.1), channel_id=1, replica_groups=mesh['vox'=32,'opt'=16] {'opt'}, use_global_device_ids=true, to_apply=%region_5.0 | all-reduce | flops 768 | bytes 6144 | tf_op jit(solution)/shard_map/psum | solution.py:43
  931.9 0.6 subtract_maximum_fusion
  (9 shorter events, 0.0 us)
Async XLA Ops:
  8.0 345.3 %all-reduce.3.cloned.1.call-start = ((), (), s32[]{:S(2)}) async-start(), calls=%async_computation.1 | async-start | bytes 2097152 | tf_op jit(solution)/shard_map/psum | solution.py:31
  9.1 39.3 %copy-start = (bf16[256,768]{1,0:T(8,128)(2,1)S(1)}, bf16[256,768]{1,0:T(8,128)(2,1)}, u32[]{:S(2)}) copy-start(bf16[256,768]{1,0:T(8,128)(2,1)} %param.7) | copy-start | bytes 1179652
  9.1 39.3 %copy-start.4 = (f32[768]{0:T(1024)S(1)}, f32[768]{0:T(1024)}, u32[]{:S(2)}) copy-start(f32[768]{0:T(1024)} %param.11) | copy-start | bytes 9220
  48.4 304.9 %copy-start.1 = (f32[32,256]{1,0:T(8,128)S(1)}, f32[32,256]{1,0:T(8,128)}, u32[]{:S(2)}) copy-start(f32[32,256]{1,0:T(8,128)} %param.8) | copy-start | bytes 98308
  48.4 304.9 %copy-start.2 = (s32[32,256]{1,0:T(8,128)S(1)}, s32[32,256]{1,0:T(8,128)}, u32[]{:S(2)}) copy-start(s32[32,256]{1,0:T(8,128)} %param.10) | copy-start | bytes 98308
  48.4 304.9 %copy-start.3 = (s32[32,256]{1,0:T(8,128)S(1)}, s32[32,256]{1,0:T(8,128)}, u32[]{:S(2)}) copy-start(s32[32,256]{1,0:T(8,128)} %param.9) | copy-start | bytes 98308
  50.0 370.8 %all-gather.2.cloned.1.call-start = ((), (), s32[]{:S(2)}) async-start(), calls=%async_computation.2 | async-start | bytes 1671168 | tf_op jit(solution)/shard_map/all_gather | solution.py:41
  50.6 732.5 %all-reduce.5.cloned.1.call-start = ((), (), s32[]{:S(2)}) async-start(), calls=%async_computation.3 | async-start | bytes 2097152 | tf_op jit(solution)/shard_map/psum | solution.py:31
Sparse Core Ops, SparseCore 0:
  50.2 303.0 all-reduce.2
  503.2 279.8 all-reduce.4
Sparse Core Ops, SparseCore 1:
  53.8 79.8 all-gather.1
